TPU v7x, 256 devices: a whole 4x4x8 slice. The times are simulated.
256 devices in a mesh: seq: 32 (over z, y), ffn: 8 (over x, core).
Axes of the slice: x: 4, y: 4, z: 8, core: 2. Of those that a mesh axis runs over, the one named last changes fastest.
Arguments:
- patches: bfloat16 [8192, 4096], P('seq'), may hold values from -100 to 100
- gate_weight: bfloat16 [4096, 7168], P('seq', 'ffn'), may hold values from -0.09375 to 0.09375
- up_weight: bfloat16 [4096, 7168], P('seq', 'ffn'), may hold values from -0.09375 to 0.09375
- down_weight: bfloat16 [4096, 7168], P('seq', 'ffn'), may hold values from -0.25 to 0.25
- key_weight: bfloat16 [4096, 1024], P(None, 'ffn'), may hold values from -0.09375 to 0.09375
- value_weight: bfloat16 [4096, 1024], P(None, 'ffn'), may hold values from -0.09375 to 0.09375
- byte_states: bfloat16 [65536, 1024], P('seq'), may hold values from -60 to 60
- byte_patch: int32 [65536], P('seq'), may hold values from 0 to 8191, as said below
- cross_query: bfloat16 [1024, 1024], P(None, 'ffn'), may hold values from -0.375 to 0.375
- self_query: bfloat16 [1024, 1024], P(None, 'ffn'), may hold values from -0.375 to 0.375
- self_key: bfloat16 [1024, 1024], P(None, 'ffn'), may hold values from -0.375 to 0.375
- self_value: bfloat16 [1024, 1024], P(None, 'ffn'), may hold values from -0.1875 to 0.1875
- cross_out: bfloat16 [1024, 1024], P('ffn'), may hold values from -0.1875 to 0.1875
- self_out: bfloat16 [1024, 1024], P('ffn'), may hold values from -0.1875 to 0.1875
Outputs:
- update: bfloat16 [65536, 1024], P('seq', 'ffn')
Inputs may be any that keep to these rules, and one draw needn't show every extreme that they name: byte_patch starts at 0, never falls, rises by at most 1 from one byte to the next and ends at 8191, so every patch is a run of one or more bytes. The bytes s * 2048 to (s + 1) * 2048 - 1 read only patches s * 256 - 23 to (s + 1) * 256 + 15; both ends are reached in every draw.
All inputs are finite; a program needn't handle non-finite values.
Results may differ from a plain program's by a relative error of at most 0.0085.
The roundings to bfloat16 on the way count: a program that leaves them out, or rounds other values in their place, can miss the bound.
Values may be sent and summed in bfloat16 or wider, within the bound.
No kernel may reach another device: no remote copies, remote signals or barrier semaphores. Data moves between devices by JAX's collectives and lax.ppermute only.
A program may use at most 128 MiB of HBM per device.

v0:
```python
import math

import jax
import jax.numpy as jnp
from jax import lax
from jax.sharding import PartitionSpec as P

HD = 64
PWIN = 8
WINDOW = 512
HALO = 23


EPS = 1e-05


def padded(value, sides, width):
    for axis, dim in sides:
        count, length = (lax.axis_size(axis), value.shape[dim])
        up = [(i, (i + 1) % count) for i in range(count - 1)]
        down = [(j, i) for i, j in up]
        last = lax.slice_in_dim(value, length - width, length, axis=dim)
        first = lax.slice_in_dim(value, 0, width, axis=dim)
        before = lax.ppermute(last, axis, up)
        after = lax.ppermute(first, axis, down)
        value = jnp.concatenate([before, value, after], axis=dim)
    return value


def shifted(value, axis, by):
    count = lax.axis_size(axis)
    pairs = [(i, i + by) for i in range(count) if 0 <= i + by < count]
    return lax.ppermute(value, axis, pairs)


def row_normalize(matrix):
    widened = matrix.astype(jnp.float32)
    return widened * lax.rsqrt(jnp.mean(widened * widened, axis=-1, keepdims=True) + EPS)


def masked_softmax(scores, key_mask):
    masked = jnp.where(key_mask, scores, -jnp.inf)
    row_max = jnp.max(masked, axis=-1, keepdims=True)
    exp_terms = jnp.exp(masked - row_max)
    return exp_terms / jnp.sum(exp_terms, axis=-1, keepdims=True)


def local(
    patches,
    gate_weight,
    up_weight,
    down_weight,
    key_weight,
    value_weight,
    byte_states,
    byte_patch,
    cross_query,
    self_query,
    self_key,
    self_value,
    cross_out,
    self_out,
):
    patch_count = patches.shape[0]
    normed = row_normalize(patches).astype(jnp.bfloat16)

    def add_rows(piece_rows):
        return jnp.dot(normed, piece_rows, preferred_element_type=jnp.float32)

    gate_sum = add_rows(lax.all_gather(gate_weight, "seq", axis=0, tiled=True))
    up_sum = add_rows(lax.all_gather(up_weight, "seq", axis=0, tiled=True))
    hidden = (jax.nn.silu(gate_sum) * up_sum).astype(jnp.bfloat16)
    ffn_out = lax.dot_general(
        hidden,
        lax.all_gather(down_weight, "seq", axis=0, tiled=True),
        (((1,), (1,)), ((), ())),
        preferred_element_type=jnp.float32,
    )
    ffn_whole = lax.psum(ffn_out, "ffn")
    global_out = (patches.astype(jnp.float32) + ffn_whole).astype(jnp.bfloat16)
    head_cols = key_weight.shape[1]
    head_count = head_cols // HD
    score_scale = 1.0 / math.sqrt(HD)
    seq_index = lax.axis_index("seq")
    keys_c = jnp.dot(global_out, key_weight, preferred_element_type=jnp.float32).astype(
        jnp.bfloat16
    )
    values_c = jnp.dot(global_out, value_weight, preferred_element_type=jnp.float32).astype(
        jnp.bfloat16
    )
    both_c = jnp.concatenate([keys_c, values_c], axis=1)
    extended = padded(both_c, (("seq", 0),), HALO)
    key_count = extended.shape[0]
    key_index = seq_index * patch_count - HALO + jnp.arange(key_count, dtype=jnp.int32)
    cross_mask = (
        (key_index[None, :] <= byte_patch[:, None])
        & (key_index[None, :] > byte_patch[:, None] - PWIN)
        & (key_index[None, :] >= 0)
    )
    byte_count = byte_states.shape[0]
    query_c = jnp.dot(byte_states, cross_query, preferred_element_type=jnp.float32).astype(
        jnp.bfloat16
    )
    query_s = jnp.dot(byte_states, self_query, preferred_element_type=jnp.float32).astype(
        jnp.bfloat16
    )
    keys_s = jnp.dot(byte_states, self_key, preferred_element_type=jnp.float32).astype(jnp.bfloat16)
    values_s = jnp.dot(byte_states, self_value, preferred_element_type=jnp.float32).astype(
        jnp.bfloat16
    )
    query_here = query_c.reshape(byte_count, head_count, HD)
    keys_here = extended[:, :head_cols].reshape(key_count, head_count, HD)
    values_here = extended[:, head_cols:].reshape(key_count, head_count, HD)
    cross_scores = (
        jnp.einsum("qhd,khd->hqk", query_here, keys_here, preferred_element_type=jnp.float32)
        * score_scale
    )
    weights_c = masked_softmax(cross_scores, cross_mask[None]).astype(jnp.bfloat16)
    context_c = jnp.einsum(
        "hqk,khd->qhd", weights_c, values_here, preferred_element_type=jnp.float32
    )
    context_c = context_c.astype(jnp.bfloat16).reshape(byte_count, head_cols)
    both_s = jnp.concatenate([keys_s, values_s], axis=1)
    tail_rows = both_s[byte_count - WINDOW :]
    before = shifted(tail_rows, "seq", 1)
    stacked = jnp.concatenate([before, both_s], axis=0)
    blocks = byte_count // WINDOW
    lower_half = stacked[:byte_count].reshape(blocks, WINDOW, 2 * head_cols)
    upper_half = stacked[WINDOW:].reshape(blocks, WINDOW, 2 * head_cols)
    key_pairs = jnp.concatenate([lower_half, upper_half], axis=1)
    window_keys = key_pairs[:, :, :head_cols].reshape(blocks, 2 * WINDOW, head_count, HD)
    window_values = key_pairs[:, :, head_cols:].reshape(blocks, 2 * WINDOW, head_count, HD)
    window_queries = query_s.reshape(blocks, WINDOW, head_count, HD)
    self_scores = (
        jnp.einsum(
            "bqhd,bkhd->bhqk", window_queries, window_keys, preferred_element_type=jnp.float32
        )
        * score_scale
    )
    query_slot = jnp.arange(WINDOW, dtype=jnp.int32)[:, None]
    key_slot = jnp.arange(2 * WINDOW, dtype=jnp.int32)[None, :]
    band_mask = (key_slot > query_slot) & (key_slot <= query_slot + WINDOW)
    block_ids = jnp.arange(blocks, dtype=jnp.int32)
    key_pos = (
        seq_index * byte_count
        - WINDOW
        + block_ids[:, None] * WINDOW
        + jnp.arange(2 * WINDOW, dtype=jnp.int32)[None, :]
    )
    self_mask = band_mask[None, None] & (key_pos >= 0)[:, None, None, :]
    weights_s = masked_softmax(self_scores, self_mask).astype(jnp.bfloat16)
    context_s = jnp.einsum(
        "bhqk,bkhd->bqhd", weights_s, window_values, preferred_element_type=jnp.float32
    )
    context_s = context_s.astype(jnp.bfloat16).reshape(byte_count, head_cols)
    partial_sum = jnp.dot(context_c, cross_out, preferred_element_type=jnp.float32) + jnp.dot(
        context_s, self_out, preferred_element_type=jnp.float32
    )
    return lax.psum_scatter(partial_sum, "ffn", scatter_dimension=1, tiled=True).astype(
        jnp.bfloat16
    )


def solution(mesh):
    placed = (
        P("seq", None),
        P("seq", "ffn"),
        P("seq", "ffn"),
        P("seq", "ffn"),
        P(None, "ffn"),
        P(None, "ffn"),
        P("seq", None),
        P("seq"),
        P(None, "ffn"),
        P(None, "ffn"),
        P(None, "ffn"),
        P(None, "ffn"),
        P("ffn", None),
        P("ffn", None),
    )
    return jax.shard_map(
        local, mesh=mesh, in_specs=placed, out_specs=P("seq", "ffn"), check_vma=False
    )
```

profile of v0, /device:TPU:1, one launch (start us, length us, event | category | flops | bytes accessed | tf_op | source)
XLA Modules:
  0.0 472.8 jit_solution(5095927345951818433)
XLA Ops:
  8.8 3.9 convolution_convert_fusion.2
  15.1 4.7 collective-permute-start.2
  20.4 4.8 %convolution_convert_fusion.3 = bf16[2048,128]{0,1:T(8,128)(2,1)} fusion(bf16[2048,1024]{1,0:T(8,128)(2,1)} %param.20, bf16[1024,128]{1,0:T(8,128)(2,1)S(1)} %copy-done.14), kind=kOutput, calls=%fused_computation.31 | convolution fusion | flops 537133056 | bytes 4980736 | tf_op jit(solution)/shard_map/dot_general | solution.py:101
  25.1 3.2 convolution_convert_fusion
  32.6 3.4 reshape.197
  36.0 3.3 pad_maximum_fusion
  39.2 2.6 reshape.191
  41.9 64.2 %all-gather.4.cloned.1.call-done = bf16[4096,896]{1,0:T(8,128)(2,1)} async-done(((bf16[128,896]{1,0:T(8,128)(2,1)}), bf16[4096,896]{1,0:T(8,128)(2,1)}) %all-gather.4.cloned.1.call-update) | async-done | bytes 7340048 | tf_op jit(solution)/shard_map/all_gather | solution.py:70
  106.1 6.4 %fusion.30 = f32[256,896]{1,0:T(8,128)} fusion(bf16[4096,896]{1,0:T(8,128)(2,1)} %all-gather.4.cloned.1.call-done, bf16[256,4096]{1,0:T(8,128)(2,1)S(1)} %copy-done.4, f32[256]{0:T(256)S(1)} %add_rsqrt_fusion), kind=kOutput, calls=%fused_computation.50 | convolution fusion | flops 1882193920 | bytes 10355712 | tf_op jit(solution)/shard_map/dot_general | solution.py:68
  112.5 86.2 %all-gather.6.cloned.1.call-done = bf16[4096,896]{1,0:T(8,128)(2,1)} async-done(((bf16[128,896]{1,0:T(8,128)(2,1)}), bf16[4096,896]{1,0:T(8,128)(2,1)}) %all-gather.6.cloned.1.call-update) | async-done | bytes 7340048 | tf_op jit(solution)/shard_map/all_gather | solution.py:71
  198.8 92.7 %all-gather.8.cloned.1.call-done = bf16[4096,896]{1,0:T(8,128)(2,1)} async-done(((bf16[128,896]{1,0:T(8,128)(2,1)}), bf16[4096,896]{1,0:T(8,128)(2,1)}) %all-gather.8.cloned.1.call-update) | async-done | bytes 7340048 | tf_op jit(solution)/shard_map/all_gather | solution.py:75
  291.4 12.0 %fusion.35 = f32[256,4096]{1,0:T(8,128)} fusion(bf16[4096,896]{1,0:T(8,128)(2,1)} %all-gather.8.cloned.1.call-done, bf16[4096,896]{1,0:T(8,128)(2,1)} %all-gather.6.cloned.1.call-done, f32[256,896]{1,0:T(8,128)} %fusion.30, bf16[256,4096]{1,0:T(8,128)(2,1)S(1)} %copy-done.4, f32[256]{0:T(256)S(1)} %add_rsqrt_fusion), kind=kOutput, calls=%fused_computation.52 | convolution fusion | flops 3762618368 | bytes 21890048 | tf_op jit(solution)/shard_map/dot_general | solution.py:73
  303.5 2.6 constant_dynamic-update-slice_fusion.1
  306.1 2.6 reshape.192
  308.8 2.6 constant_dynamic-update-slice_fusion
  311.3 2.6 fusion.51
  316.6 11.0 %fusion.54 = (f32[4,2,512]{2,1,0:T(2,128)S(1)}, f32[4,2,512,1024]{3,2,1,0:T(8,128)}) fusion(pred[4,512,1024]{2,1,0:T(8,128)(4,1)} %broadcast_and_fusion, bf16[4,1024,2,64]{1,3,2,0:T(8,128)(2,1)} %bitcast.47, bf16[4,512,2,64]{3,2,1,0:T(2,128)(2,1)} %reshape.197), kind=kOutput, calls=%fused_computation.79 | convolution fusion | flops 553649152 | bytes 20463616 | tf_op jit(solution)/shard_map/sub | solution.py:44
  327.6 49.4 %all-reduce.2.cloned.1.call-done = f32[256,4096]{1,0:T(8,128)} async-done(((f32[256,4096]{1,0:T(8,128)}), f32[256,4096]{1,0:T(8,128)}) %all-reduce.2.cloned.1.call-update) | async-done | bytes 4194320 | tf_op jit(solution)/shard_map/psum | solution.py:79
  377.0 3.1 convolution_convert_fusion.4
  381.7 3.1 collective-permute-start
  386.4 8.6 %fusion.21 = bf16[4,512,2,64]{1,3,2,0:T(8,128)(2,1)S(1)} fusion(bf16[4,1024,2,64]{1,3,2,0:T(8,128)(2,1)S(1)} %bitcast.46, f32[4,2,512,1024]{3,2,1,0:T(8,128)} %get-tuple-element.14, f32[4,2,512]{2,1,0:T(2,128)S(1)} %get-tuple-element.13), kind=kOutput, calls=%fused_computation.39 | convolution fusion | flops 545521664 | bytes 18366464 | tf_op jit(solution)/shard_map/bhqk,bkhd->bqhd/dot_general | solution.py:152
  397.6 2.5 fusion.15
  401.5 4.5 convolution_add_fusion
  406.0 58.2 %reduce-scatter.2.cloned.1.call-done = f32[2048,128]{1,0:T(8,128)} async-done(((f32[2048,1024]{1,0:T(8,128)}), f32[2048,128]{1,0:T(8,128)}) %reduce-scatter.2.cloned.1.call-update) | async-done | bytes 1048592 | tf_op jit(solution)/shard_map/reduce_scatter | solution.py:159
  (72 shorter events, 21.1 us)
Async XLA Ops:
  6.5 370.5 %copy-start = (bf16[4096,128]{1,0:T(8,128)(2,1)S(1)}, bf16[4096,128]{1,0:T(8,128)(2,1)}, u32[]{:S(2)}) copy-start(bf16[4096,128]{1,0:T(8,128)(2,1)} %param.19) | copy-start | bytes 3145732
  6.5 6.1 %copy-start.13 = (bf16[1024,128]{1,0:T(8,128)(2,1)S(1)}, bf16[1024,128]{1,0:T(8,128)(2,1)}, u32[]{:S(2)}) copy-start(bf16[1024,128]{1,0:T(8,128)(2,1)} %param.25) | copy-start | bytes 786436
  6.5 99.6 %all-gather.4.cloned.1.call-start = ((), (), s32[]{:S(2)}) async-start(), calls=%async_computation.1 | async-start | bytes 7569408 | tf_op jit(solution)/shard_map/all_gather | solution.py:70
  7.3 191.5 %all-gather.6.cloned.1.call-start = ((), (), s32[]{:S(2)}) async-start(), calls=%async_computation.2 | async-start | bytes 7569408 | tf_op jit(solution)/shard_map/all_gather | solution.py:71
  8.0 283.4 %all-gather.8.cloned.1.call-start = ((), (), s32[]{:S(2)}) async-start(), calls=%async_computation.3 | async-start | bytes 7569408 | tf_op jit(solution)/shard_map/all_gather | solution.py:75
  8.7 368.3 %all-reduce.2.cloned.1.call-start = ((), (), s32[]{:S(2)}) async-start(), calls=%async_computation.4 | async-start | bytes 8388608 | tf_op jit(solution)/shard_map/psum | solution.py:79
  8.8 3.9 copy-start.2
  12.7 1.6 copy-start.6
  12.7 7.2 %copy-start.16 = (s32[2048]{0:T(1024)S(1)}, s32[2048]{0:T(1024)}, u32[]{:S(2)}) copy-start(s32[2048]{0:T(1024)} %param.21) | copy-start | bytes 24580
  12.7 7.6 %copy-start.14 = (bf16[1024,128]{1,0:T(8,128)(2,1)S(1)}, bf16[1024,128]{1,0:T(8,128)(2,1)}, u32[]{:S(2)}) copy-start(bf16[1024,128]{1,0:T(8,128)(2,1)} %param.22) | copy-start | bytes 786436
  15.1 20.8 %collective-permute-start.2 = (bf16[512,256]{0,1:T(8,128)(2,1)S(1)}, bf16[512,256]{0,1:T(8,128)(2,1)}, u32[]{:S(2)}, u32[]{:S(2)}) collective-permute-start(bf16[512,256]{0,1:T(8,128)(2,1)S(1)} %fusion.38), channel_id=1, source_target_pairs={{0,8},{8,16},{16,24},{24,32},{32,40},{40,48},{48,56},{56,64},{64,7... | collective-permute-start | bytes 786440 | tf_op jit(solution)/shard_map/ppermute | solution.py:33
  19.8 5.3 %copy-start.3 = (bf16[2048,1024]{1,0:T(8,128)(2,1)S(1)}, bf16[2048,1024]{1,0:T(8,128)(2,1)}, u32[]{:S(2)}) copy-start(bf16[2048,1024]{1,0:T(8,128)(2,1)} %param.20) | copy-start | bytes 12582916
  25.1 7.0 %copy-start.4 = (bf16[256,4096]{1,0:T(8,128)(2,1)S(1)}, bf16[256,4096]{1,0:T(8,128)(2,1)}, u32[]{:S(2)}) copy-start(bf16[256,4096]{1,0:T(8,128)(2,1)} %param.14) | copy-start | bytes 6291460
  303.5 160.7 %reduce-scatter.2.cloned.1.call-start = ((), (), s32[]{:S(2)}) async-start(), calls=%async_computation.5 | async-start | bytes 9437184 | tf_op jit(solution)/shard_map/reduce_scatter | solution.py:159
  377.0 3.4 copy-start.5
  377.0 3.7 copy-start.8
  380.8 5.7 %copy-start.9 = (bf16[4,1024,128]{1,2,0:T(8,128)(2,1)S(1)}, bf16[4,1024,128]{1,2,0:T(8,128)(2,1)}, u32[]{:S(2)}) copy-start(bf16[4,1024,128]{1,2,0:T(8,128)(2,1)} %copy.18) | copy-start | bytes 3145732
  381.7 13.8 %collective-permute-start = (bf16[23,256]{0,1:T(8,128)(2,1)S(1)}, bf16[23,256]{0,1:T(8,128)(2,1)S(1)}, u32[]{:S(2)}, u32[]{:S(2)}) collective-permute-start(bf16[23,256]{0,1:T(8,128)(2,1)S(1)} %get-tuple-element.11), channel_id=1, source_target_pairs={{0,8},{8,16},{16,24},{24,32},{32,40},{40,48},{48,56},{56,64},{64,7... | collective-permute-start | bytes 35336 | tf_op jit(solution)/shard_map/ppermute | solution.py:24
  384.8 10.7 %collective-permute-start.1 = (bf16[23,256]{0,1:T(8,128)(2,1)S(1)}, bf16[23,256]{0,1:T(8,128)(2,1)S(1)}, u32[]{:S(2)}, u32[]{:S(2)}) collective-permute-start(bf16[23,256]{0,1:T(8,128)(2,1)S(1)} %get-tuple-element.12), channel_id=1, source_target_pairs={{8,0},{16,8},{24,16},{32,24},{40,32},{48,40},{56,48},{64,56},{72,6... | collective-permute-start | bytes 35336 | tf_op jit(solution)/shard_map/ppermute | solution.py:25
  386.4 9.3 %copy-start.10 = (pred[2048,302]{0,1:T(8,128)(4,1)S(1)}, pred[2048,302]{0,1:T(8,128)(4,1)}, u32[]{:S(2)}) copy-start(pred[2048,302]{0,1:T(8,128)(4,1)} %and_and_fusion) | copy-start | bytes 1855492
  386.4 9.3 %copy-start.11 = (bf16[2048,128]{0,1:T(8,128)(2,1)S(1)}, bf16[2048,128]{0,1:T(8,128)(2,1)}, u32[]{:S(2)}) copy-start(bf16[2048,128]{0,1:T(8,128)(2,1)} %convolution_convert_fusion.3) | copy-start | bytes 1572868
  397.6 2.5 copy-start.15
  400.2 1.3 copy-start.12
  406.0 60.3 %copy-start.1 = (bf16[4096,128]{1,0:T(8,128)(2,1)S(1)}, bf16[4096,128]{1,0:T(8,128)(2,1)}, u32[]{:S(2)}) copy-start(bf16[4096,128]{1,0:T(8,128)(2,1)} %param.19) | copy-start | bytes 3145732
  (1 other events, 0.8 us)
Sparse Core Ops, SparseCore 0:
  9.9 96.1 all-gather.3
  108.7 90.0 all-gather.5
  201.3 90.0 all-gather.7
  303.6 73.3 all-reduce.1
  406.1 58.0 reduce-scatter.1
where the time goes:
time: 473 us
  waiting for transfers between devices  353 us (75%)
  matrix products  65.5 us (14%)
  local copies, waits for them, and re-layouts  21.1 us (4%)
  between operations  13.5 us (3%)
  other arithmetic  10.4 us (2%)
  starting transfers between devices  9.53 us (2%)
    all_gather x1, waiting for transfers between devices, local(): lax.all_gather(down_weight, 'seq', axis=0, tiled=True)  92.7 us
    all_gather x1, waiting for transfers between devices, local(): up_sum = add_rows(lax.all_gather(up_weight, 'seq', axis=0, tiled=True))  86.2 us
    all_gather x1, waiting for transfers between devices, local(): gate_sum = add_rows(lax.all_gather(gate_weight, 'seq', axis=0, tiled=True))  64.2 us
    reduce_scatter x1, waiting for transfers between devices, local(): lax.psum_scatter(partial_sum, 'ffn', scatter_dimension=1, tiled=True)  58.2 us
    psum x1, waiting for transfers between devices, local(): ffn_whole = lax.psum(ffn_out, 'ffn')  49.4 us
    sub x2, matrix products, masked_softmax(): exp_terms = jnp.exp(masked - row_max)  12.8 us
    dot_general x1, matrix products, local(): lax.dot_general(hidden, lax.all_gather(down_weight, 'seq', axis=0, tiled=...  12 us
  transfers between devices with their start and end apart: 8, of which 5 were waited for; matrix products, arithmetic and copies ran while one was open for 14% of the time, Pallas kernels for 0%

commit v1 on v0

v1 whole, which is shorter than its diff:
```python
import math

import jax
import jax.numpy as jnp
from jax import lax
from jax.sharding import Mesh, PartitionSpec as P

HD = 64
PWIN = 8
WINDOW = 512
HALO = 23
EPS = 1e-05

NZ, NY, NX, NC = 8, 4, 4, 2
NF = NX * NC
SEQ = ("z", "y")
FFN = ("x", "c")
BF = jnp.bfloat16
F32 = jnp.float32


def swap(value, axes):
    return lax.all_to_all(value, axes, split_axis=0, concat_axis=0, tiled=True)


def spread(value, axes, count):
    return swap(jnp.broadcast_to(value[None], (count,) + value.shape), axes)


def row_normalize(matrix):
    widened = matrix.astype(F32)
    return widened * lax.rsqrt(jnp.mean(widened * widened, axis=-1, keepdims=True) + EPS)


def masked_softmax(scores, key_mask):
    masked = jnp.where(key_mask, scores, -jnp.inf)
    row_max = jnp.max(masked, axis=-1, keepdims=True)
    exp_terms = jnp.exp(masked - row_max)
    return exp_terms / jnp.sum(exp_terms, axis=-1, keepdims=True)


def with_halo(value, width):
    count, length = NZ * NY, value.shape[0]
    up = [(i, i + 1) for i in range(count - 1)]
    down = [(j, i) for i, j in up]
    before = lax.ppermute(value[length - width :], SEQ, up)
    after = lax.ppermute(value[:width], SEQ, down)
    return jnp.concatenate([before, value, after], axis=0)


def local(
    patches,
    gate_weight,
    up_weight,
    down_weight,
    key_weight,
    value_weight,
    byte_states,
    byte_patch,
    cross_query,
    self_query,
    self_key,
    self_value,
    cross_out,
    self_out,
):
    y = lax.axis_index("y")
    core = lax.axis_index("c")
    seq_index = lax.axis_index(SEQ)
    rows, width = patches.shape
    d_rows, hid = gate_weight.shape
    hid_y = hid // NY
    hid_z = hid // NZ
    pad_y = -hid_y % 128
    slot = hid_y + pad_y
    head_cols = key_weight.shape[1]
    both_cols = 2 * head_cols

    def by_y(weight):
        pieces = weight.reshape(d_rows, NY, hid_y).transpose(1, 0, 2)
        return jnp.pad(pieces, ((0, 0), (0, 0), (0, pad_y)))

    gate_up = swap(jnp.concatenate([by_y(gate_weight), by_y(up_weight)], axis=2), "y")
    gate_up = lax.all_gather(gate_up.reshape(NY * d_rows, 2 * slot), "z", axis=0, tiled=True)

    normed = row_normalize(patches).astype(BF)
    half = rows // NC
    own_half = lax.dynamic_slice_in_dim(normed, core * half, half, axis=0)
    group = spread(spread(own_half, "y", NY), "c", NC)
    group = group.reshape(NC * NY * half, width)

    kv_weight = jnp.concatenate([key_weight, value_weight], axis=1)
    kv_rows = lax.dynamic_index_in_dim(
        kv_weight.reshape(NZ, NY, d_rows, both_cols), y, axis=1, keepdims=False
    ).reshape(NZ * d_rows, both_cols)
    kv_all = spread(kv_rows, FFN, NF).reshape(NF, NZ * d_rows, both_cols)
    down_t = swap(down_weight.T.reshape(NZ, hid_z, d_rows), "z")
    down_t = down_t.reshape(NZ, hid_z, d_rows).transpose(1, 0, 2).reshape(hid_z, NZ * d_rows)
    mix = jnp.einsum("hd,fdc->fhc", down_t, kv_all, preferred_element_type=F32)
    mix = swap(mix.reshape(NY, NF // NY * hid_z, both_cols), "y")
    mix = jnp.sum(mix, axis=0).astype(BF)
    mix = lax.all_gather(mix, SEQ, axis=0, tiled=True)
    mix = mix.reshape(NY, NZ // NY, NY, NF // NY, hid_z, both_cols).transpose(2, 3, 0, 1, 4, 5)
    mix = mix.reshape(NF, NY, hid_y, both_cols)
    mix = jnp.pad(mix, ((0, 0), (0, 0), (0, pad_y), (0, 0)))

    own_kv = jnp.dot(patches, kv_weight, preferred_element_type=F32)

    byte_count = byte_states.shape[0]
    head_count = head_cols // HD
    score_scale = 1.0 / math.sqrt(HD)

    def project(weight):
        return jnp.dot(byte_states, weight, preferred_element_type=F32).astype(BF)

    keys_s, values_s = project(self_key), project(self_value)
    both_s = jnp.concatenate([keys_s, values_s], axis=1)
    count = NZ * NY
    before = lax.ppermute(
        both_s[byte_count - WINDOW :], SEQ, [(i, i + 1) for i in range(count - 1)]
    )
    query_s = project(self_query)
    query_c = project(cross_query)
    stacked = jnp.concatenate([before, both_s], axis=0)
    blocks = byte_count // WINDOW
    lower_half = stacked[:byte_count].reshape(blocks, WINDOW, both_cols)
    upper_half = stacked[WINDOW:].reshape(blocks, WINDOW, both_cols)
    key_pairs = jnp.concatenate([lower_half, upper_half], axis=1)
    window_keys = key_pairs[:, :, :head_cols].reshape(blocks, 2 * WINDOW, head_count, HD)
    window_values = key_pairs[:, :, head_cols:].reshape(blocks, 2 * WINDOW, head_count, HD)
    window_queries = query_s.reshape(blocks, WINDOW, head_count, HD)
    self_scores = (
        jnp.einsum("bqhd,bkhd->bhqk", window_queries, window_keys, preferred_element_type=F32)
        * score_scale
    )
    query_slot = jnp.arange(WINDOW, dtype=jnp.int32)[:, None]
    key_slot = jnp.arange(2 * WINDOW, dtype=jnp.int32)[None, :]
    band_mask = (key_slot > query_slot) & (key_slot <= query_slot + WINDOW)
    block_ids = jnp.arange(blocks, dtype=jnp.int32)
    key_pos = (
        seq_index * byte_count
        - WINDOW
        + block_ids[:, None] * WINDOW
        + jnp.arange(2 * WINDOW, dtype=jnp.int32)[None, :]
    )
    self_mask = band_mask[None, None] & (key_pos >= 0)[:, None, None, :]
    weights_s = masked_softmax(self_scores, self_mask).astype(BF)
    context_s = jnp.einsum(
        "bhqk,bkhd->bqhd", weights_s, window_values, preferred_element_type=F32
    )
    context_s = context_s.astype(BF).reshape(NF, byte_count // NF, head_cols)
    context_s = swap(context_s, FFN)
    outs = spread(jnp.stack([cross_out, self_out]), FFN, NF)
    outs = outs.reshape(NF, 2, head_cols, NF, head_cols)
    self_part = jnp.einsum(
        "frd,fdgo->gro", context_s, outs[:, 1], preferred_element_type=F32
    )

    sums = jnp.dot(group, gate_up, preferred_element_type=F32)
    hidden = (jax.nn.silu(sums[:, :slot]) * sums[:, slot:]).astype(BF)
    hidden = hidden.reshape(NC, NY, half, slot).transpose(1, 0, 2, 3).reshape(NY, rows, slot)
    hidden = swap(hidden, "y")
    part = jnp.einsum("yrk,fykc->frc", hidden, mix, preferred_element_type=F32).astype(BF)
    part = swap(part, FFN)
    both_c = (own_kv + jnp.sum(part.astype(F32), axis=0)).astype(BF)

    extended = with_halo(both_c, HALO)
    key_count = extended.shape[0]
    key_index = seq_index * rows - HALO + jnp.arange(key_count, dtype=jnp.int32)
    cross_mask = (
        (key_index[None, :] <= byte_patch[:, None])
        & (key_index[None, :] > byte_patch[:, None] - PWIN)
        & (key_index[None, :] >= 0)
    )
    query_here = query_c.reshape(byte_count, head_count, HD)
    keys_here = extended[:, :head_cols].reshape(key_count, head_count, HD)
    values_here = extended[:, head_cols:].reshape(key_count, head_count, HD)
    cross_scores = (
        jnp.einsum("qhd,khd->hqk", query_here, keys_here, preferred_element_type=F32)
        * score_scale
    )
    weights_c = masked_softmax(cross_scores, cross_mask[None]).astype(BF)
    context_c = jnp.einsum("hqk,khd->qhd", weights_c, values_here, preferred_element_type=F32)
    context_c = context_c.astype(BF).reshape(NF, byte_count // NF, head_cols)
    context_c = swap(context_c, FFN)
    update = self_part + jnp.einsum(
        "frd,fdgo->gro", context_c, outs[:, 0], preferred_element_type=F32
    )
    return swap(update.astype(BF), FFN).reshape(byte_count, head_cols)


def solution(mesh):
    fine = Mesh(mesh.devices.reshape(NZ, NY, NX, NC), SEQ + FFN)
    placed = (
        P(SEQ, None),
        P(SEQ, FFN),
        P(SEQ, FFN),
        P(SEQ, FFN),
        P(None, FFN),
        P(None, FFN),
        P(SEQ, None),
        P(SEQ),
        P(None, FFN),
        P(None, FFN),
        P(None, FFN),
        P(None, FFN),
        P(FFN, None),
        P(FFN, None),
    )
    return jax.shard_map(
        local, mesh=fine, in_specs=placed, out_specs=P(SEQ, FFN), check_vma=False
    )
```

time: 473 us -> 371 us (0.78)
  waiting for transfers between devices: 353 us -> 111 us
  blocking collectives: 0 us -> 47 us
  starting transfers between devices: 9.53 us -> 55.9 us
  local copies, waits for them, and re-layouts: 21.1 us -> 62.1 us
  other arithmetic: 10.4 us -> 19.6 us
  matrix products: 65.5 us -> 59 us
    all_gather x3 -> x2, waiting for transfers between devices: 243 us -> 0.01 us  [the longest x1 0.01 us: local(): lax.all_gather(gate_up.reshape(NY * d_rows, 2 * slot), 'z', axis=0, tiled...]
    all_to_all x0 -> x9, waiting for transfers between devices: none -> 110 us  [swap(): return lax.all_to_all(value, axes, split_axis=0, concat_axis=0, tiled=True)]
    reduce_scatter x1 -> x0, waiting for transfers between devices: 58.2 us -> none  [local(): lax.psum_scatter(partial_sum, 'ffn', scatter_dimension=1, tiled=True)]
    psum x1 -> x0, waiting for transfers between devices: 49.4 us -> none  [local(): ffn_whole = lax.psum(ffn_out, 'ffn')]
    all_to_all x0 -> x9, starting transfers between devices: none -> 48.8 us  [swap(): return lax.all_to_all(value, axes, split_axis=0, concat_axis=0, tiled=True)]
    all_to_all x0 -> x3, blocking collectives: none -> 47 us  [swap(): return lax.all_to_all(value, axes, split_axis=0, concat_axis=0, tiled=True)]
    broadcast_in_dim x0 -> x4, local copies, waits for them, and re-layouts: none -> 16.4 us  [spread(): return swap(jnp.broadcast_to(value[None], (count,) + value.shape), axes)]
    reshape x2 -> x7, local copies, waits for them, and re-layouts: 5.28 us -> 16.6 us  [the longest x1 6.3 us: local(): mix = mix.reshape(NF, NY, hid_y, both_cols)]
  transfers between devices with their start and end apart: 8 -> 14, of which waited for: 5 -> 8; matrix products, arithmetic and copies ran while one was open for 14% -> 35% of each run, Pallas kernels for 0% -> 0%
where the time goes in v1:
time: 371 us; the launch traced here: 369 us
  waiting for transfers between devices  111 us (30%)
  local copies, waits for them, and re-layouts  62.1 us (17%)
  matrix products  59 us (16%)
  starting transfers between devices  55.9 us (15%)
  blocking collectives  47 us (13%)
  other arithmetic  19.6 us (5%)
  between operations  13.8 us (4%)
    all_to_all x9, waiting for transfers between devices, swap(): return lax.all_to_all(value, axes, split_axis=0, concat_axis=0, tiled=True)  110 us
    all_to_all x9, starting transfers between devices, swap(): return lax.all_to_all(value, axes, split_axis=0, concat_axis=0, tiled=True)  48.8 us
    all_to_all x3, blocking collectives, swap(): return lax.all_to_all(value, axes, split_axis=0, concat_axis=0, tiled=True)  47 us
    broadcast_in_dim x4, local copies, waits for them, and re-layouts, spread(): return swap(jnp.broadcast_to(value[None], (count,) + value.shape), axes)  16.4 us
    sub x2, matrix products, masked_softmax(): exp_terms = jnp.exp(masked - row_max)  12.6 us
    dot_general x4, matrix products, project(): return jnp.dot(byte_states, weight, preferred_element_type=F32).astype(BF)  12.2 us
    dot_general x1, matrix products, local(): jnp.einsum('bhqk,bkhd->bqhd', weights_s, window_values, preferred_element...  9.29 us
    dot_general x1, matrix products, local(): sums = jnp.dot(group, gate_up, preferred_element_type=F32)  8.37 us
  transfers between devices with their start and end apart: 14, of which 8 were waited for; matrix products, arithmetic and copies ran while one was open for 35% of the time, Pallas kernels for 0%

profile of v1, /device:TPU:1, one launch (start us, length us, event | category | flops | bytes accessed | tf_op | source)
XLA Modules:
  0.0 368.6 jit_solution(205238868070925682)
XLA Ops:
  8.9 13.4 %all_to_all.60 = bf16[4,128,512]{1,2,0:T(8,128)(2,1)S(1)} all-to-all(bf16[4,128,512]{1,2,0:T(8,128)(2,1)S(1)} %fusion.47), channel_id=1, replica_groups=mesh['z'=8,'y'=4,'x'=4,'c'=2] {'y'}, dimensions={0} | all-to-all | bytes 1048576 | tf_op jit(solution)/shard_map/all_to_all | solution.py:23
  24.2 8.2 %all-to-all-start.3 = ((bf16[8,112,128]{2,1,0:T(8,128)(2,1)}), bf16[8,112,128]{2,1,0:T(8,128)(2,1)S(1)}, u32[]{:S(2)}, u32[]{:S(2)}) async-start(bf16[8,112,128]{2,1,0:T(8,128)(2,1)} %bitcast.15), calls=%async_computation.3 | async-start | bytes 458752 | tf_op jit(solution)/shard_map/all_to_all | solution.py:23
  34.3 7.2 %all-to-all-done.3 = bf16[8,112,128]{2,1,0:T(8,128)(2,1)S(1)} async-done(((bf16[8,112,128]{2,1,0:T(8,128)(2,1)}), bf16[8,112,128]{2,1,0:T(8,128)(2,1)S(1)}, u32[]{:S(2)}, u32[]{:S(2)}) %all-to-all-start.3) | async-done | bytes 229408 | tf_op jit(solution)/shard_map/all_to_all | solution.py:23
  43.8 8.8 %all-to-all-start.2 = ((bf16[8,1024,256]{2,1,0:T(8,128)(2,1)}), bf16[8,1024,256]{2,1,0:T(8,128)(2,1)}, u32[]{:S(2)}, u32[]{:S(2)}) async-start(bf16[8,1024,256]{2,1,0:T(8,128)(2,1)} %broadcast_in_dim.34), calls=%async_computation.2 | async-start | bytes 8388608 | tf_op jit(solution)/shard_map/all_to_all | solution.py:23
  74.3 27.1 %all-to-all-done.2 = bf16[8,1024,256]{2,1,0:T(8,128)(2,1)} async-done(((bf16[8,1024,256]{2,1,0:T(8,128)(2,1)}), bf16[8,1024,256]{2,1,0:T(8,128)(2,1)}, u32[]{:S(2)}, u32[]{:S(2)}) %all-to-all-start.2) | async-done | bytes 4194336 | tf_op jit(solution)/shard_map/all_to_all | solution.py:23
  112.3 10.1 %all-to-all-done.4 = f32[4,224,256]{2,1,0:T(8,128)} async-done(((f32[4,224,256]{2,1,0:T(8,128)}), f32[4,224,256]{2,1,0:T(8,128)}, u32[]{:S(2)}, u32[]{:S(2)}) %all-to-all-start.4) | async-done | bytes 917536 | tf_op jit(solution)/shard_map/all_to_all | solution.py:23
  126.1 4.9 %all-to-all-start.5 = ((bf16[4,128,4096]{2,1,0:T(8,128)(2,1)}), bf16[4,128,4096]{2,1,0:T(8,128)(2,1)}, u32[]{:S(2)}, u32[]{:S(2)}) async-start(bf16[4,128,4096]{2,1,0:T(8,128)(2,1)} %broadcast_in_dim.35), calls=%async_computation.5 | async-start | bytes 8388608 | tf_op jit(solution)/shard_map/all_to_all | solution.py:23
  149.0 10.8 %fusion.65 = (f32[4,2,512]{2,1,0:T(2,128)S(1)}, f32[4,2,512,1024]{3,2,1,0:T(8,128)}) fusion(pred[4,512,1024]{2,1,0:T(8,128)(4,1)} %broadcast_and_fusion, bf16[4,1024,2,64]{1,3,2,0:T(8,128)(2,1)} %bitcast.130, bf16[4,512,2,64]{3,2,1,0:T(2,128)(2,1)S(1)} %copy-done.6), kind=kOutput, calls=%fused_computation.96 | convolution fusion | flops 553649152 | bytes 20463616 | tf_op jit(solution)/shard_map/sub | solution.py:38
  159.8 20.2 %all-to-all-done.5 = bf16[4,128,4096]{2,1,0:T(8,128)(2,1)} async-done(((bf16[4,128,4096]{2,1,0:T(8,128)(2,1)}), bf16[4,128,4096]{2,1,0:T(8,128)(2,1)}, u32[]{:S(2)}, u32[]{:S(2)}) %all-to-all-start.5) | async-done | bytes 4194336 | tf_op jit(solution)/shard_map/all_to_all | solution.py:23
  180.0 6.5 %broadcast_in_dim.36 = bf16[2,4,128,4096]{3,2,1,0:T(8,128)(2,1)} broadcast(bf16[4,128,4096]{2,1,0:T(8,128)(2,1)} %all-to-all-done.5), dimensions={1,2,3} | broadcast | bytes 12582912 | tf_op jit(solution)/shard_map/broadcast_in_dim | solution.py:27
  186.5 20.8 %all_to_all.61 = bf16[2,4,128,4096]{3,2,1,0:T(8,128)(2,1)} all-to-all(bf16[2,4,128,4096]{3,2,1,0:T(8,128)(2,1)} %broadcast_in_dim.36), channel_id=1, replica_groups=mesh['z'=8,'y'=4,'x'=4,'c'=2] {'c'}, dimensions={0} | all-to-all | bytes 16777216 | tf_op jit(solution)/shard_map/all_to_all | solution.py:23
  207.3 8.4 %fusion.71 = f32[1024,512]{1,0:T(8,128)S(1)} fusion(bf16[1024,4096]{1,0:T(8,128)(2,1)} %bitcast.121, bf16[4096,512]{1,0:T(8,128)(2,1)} %all-gather.5.cloned.1.call-done), kind=kOutput, calls=%fused_computation.98 | convolution fusion | flops 4294967296 | bytes 14680064 | tf_op jit(solution)/shard_map/dot_general | solution.py:159
  216.8 4.4 %all-to-all-start.8 = ((bf16[4,256,256]{2,1,0:T(8,128)(2,1)}), bf16[4,256,256]{2,1,0:T(8,128)(2,1)}, u32[]{:S(2)}, u32[]{:S(2)}) async-start(bf16[4,256,256]{2,1,0:T(8,128)(2,1)} %bitcast.30), calls=%async_computation.8 | async-start | bytes 1048576 | tf_op jit(solution)/shard_map/all_to_all | solution.py:23
  221.2 9.3 %fusion.32 = bf16[4,512,2,64]{1,3,2,0:T(8,128)(2,1)} fusion(bf16[4,1024,2,64]{1,3,2,0:T(8,128)(2,1)S(1)} %bitcast.129, f32[4,2,512,1024]{3,2,1,0:T(8,128)} %get-tuple-element.16, f32[4,2,512]{2,1,0:T(2,128)S(1)} %get-tuple-element.15), kind=kOutput, calls=%fused_computation.47 | convolution fusion | flops 545521664 | bytes 18366464 | tf_op jit(solution)/shard_map/bhqk,bkhd->bqhd/dot_general | solution.py:148
  237.9 4.3 %copy.55 = bf16[4,2,4,2,112,256]{5,4,3,2,1,0:T(8,128)(2,1)} copy(bf16[4,2,4,2,112,256]{5,4,1,0,3,2:T(8,128)(2,1)} %bitcast.123) | data formatting | bytes 7340032 | tf_op jit(solution)/shard_map/transpose | solution.py:103
  242.2 6.3 %copy.56 = bf16[8,4,224,256]{2,3,1,0:T(8,128)(2,1)} copy(bf16[8,4,224,256]{3,2,1,0:T(8,128)(2,1)} %bitcast.120) | data formatting | bytes 7340032 | tf_op jit(solution)/shard_map/reshape | solution.py:104
  248.5 4.6 %fusion.25 = bf16[8,256,256]{1,2,0:T(8,128)(2,1)} fusion(bf16[8,4,224,256]{2,3,1,0:T(8,128)(2,1)} %copy.56, bf16[4,256,256]{2,1,0:T(8,128)(2,1)} %all-to-all-done.8), kind=kOutput, calls=%fused_computation.42 | convolution fusion | flops 1074266112 | bytes 5242880 | tf_op jit(solution)/shard_map/yrk,fykc->frc/dot_general | solution.py:163
  253.9 4.8 %all-to-all-start.9 = ((bf16[8,256,256]{1,2,0:T(8,128)(2,1)}), bf16[8,256,256]{1,2,0:T(8,128)(2,1)S(1)}, u32[]{:S(2)}, u32[]{:S(2)}) async-start(bf16[8,256,256]{1,2,0:T(8,128)(2,1)} %fusion.25), calls=%async_computation.9 | async-start | bytes 2097152 | tf_op jit(solution)/shard_map/all_to_all | solution.py:23
  262.7 11.1 %all-to-all-done.9 = bf16[8,256,256]{1,2,0:T(8,128)(2,1)S(1)} async-done(((bf16[8,256,256]{1,2,0:T(8,128)(2,1)}), bf16[8,256,256]{1,2,0:T(8,128)(2,1)S(1)}, u32[]{:S(2)}, u32[]{:S(2)}) %all-to-all-start.9) | async-done | bytes 1048608 | tf_op jit(solution)/shard_map/all_to_all | solution.py:23
  277.6 5.5 %all-to-all-start = ((bf16[8,2,128,1024]{2,3,1,0:T(8,128)(2,1)}), bf16[8,2,128,1024]{2,3,1,0:T(8,128)(2,1)}, u32[]{:S(2)}, u32[]{:S(2)}) async-start(bf16[8,2,128,1024]{2,3,1,0:T(8,128)(2,1)} %broadcast_in_dim.30), calls=%async_computation | async-start | bytes 8388608 | tf_op jit(solution)/shard_map/all_to_all | solution.py:23
  301.7 30.2 %all-to-all-done = bf16[8,2,128,1024]{2,3,1,0:T(8,128)(2,1)} async-done(((bf16[8,2,128,1024]{2,3,1,0:T(8,128)(2,1)}), bf16[8,2,128,1024]{2,3,1,0:T(8,128)(2,1)}, u32[]{:S(2)}, u32[]{:S(2)}) %all-to-all-start) | async-done | bytes 4194336 | tf_op jit(solution)/shard_map/all_to_all | solution.py:23
  332.0 4.4 %all-to-all-start.10 = ((bf16[8,256,128]{2,1,0:T(8,128)(2,1)}), bf16[8,256,128]{2,1,0:T(8,128)(2,1)S(1)}, u32[]{:S(2)}, u32[]{:S(2)}) async-start(bf16[8,256,128]{2,1,0:T(8,128)(2,1)} %copy.64), calls=%async_computation.10 | async-start | bytes 1048576 | tf_op jit(solution)/shard_map/all_to_all | solution.py:23
  341.2 4.5 %all-to-all-done.10 = bf16[8,256,128]{2,1,0:T(8,128)(2,1)S(1)} async-done(((bf16[8,256,128]{2,1,0:T(8,128)(2,1)}), bf16[8,256,128]{2,1,0:T(8,128)(2,1)S(1)}, u32[]{:S(2)}, u32[]{:S(2)}) %all-to-all-start.10) | async-done | bytes 524320 | tf_op jit(solution)/shard_map/all_to_all | solution.py:23
  348.0 12.7 %all_to_all.62 = bf16[8,256,128]{1,2,0:T(8,128)(2,1)S(1)} all-to-all(bf16[8,256,128]{1,2,0:T(8,128)(2,1)S(1)} %fusion.31), channel_id=1, replica_groups=mesh['z'=8,'y'=4,'x'=4,'c'=2] {'x','c'}, dimensions={0} | all-to-all | bytes 1048576 | tf_op jit(solution)/shard_map/all_to_all | solution.py:23
  (115 shorter events, 106.4 us)
Async XLA Ops:
  6.5 46.0 %copy-start = (bf16[1024,128]{1,0:T(8,128)(2,1)S(1)}, bf16[1024,128]{1,0:T(8,128)(2,1)}, u32[]{:S(2)}) copy-start(bf16[1024,128]{1,0:T(8,128)(2,1)} %param.25) | copy-start | bytes 786436
  6.5 16.9 %copy-start.15 = (bf16[128,896]{1,0:T(8,128)(2,1)S(1)}, bf16[128,896]{1,0:T(8,128)(2,1)}, u32[]{:S(2)}) copy-start(bf16[128,896]{1,0:T(8,128)(2,1)} %param.17) | copy-start | bytes 688132
  6.5 25.9 %copy-start.7 = (bf16[4096,128]{1,0:T(8,128)(2,1)S(1)}, bf16[4096,128]{1,0:T(8,128)(2,1)}, u32[]{:S(2)}) copy-start(bf16[4096,128]{1,0:T(8,128)(2,1)} %param.18) | copy-start | bytes 3145732
  6.5 200.8 %all-gather.5.cloned.1.call-start = ((), (), s32[]{:S(2)}) async-start(), calls=%async_computation.13 | async-start | bytes 4718592 | tf_op jit(solution)/shard_map/all_gather | solution.py:84
  23.4 9.3 %copy-start.8 = (bf16[4096,128]{1,0:T(8,128)(2,1)S(1)}, bf16[4096,128]{1,0:T(8,128)(2,1)}, u32[]{:S(2)}) copy-start(bf16[4096,128]{1,0:T(8,128)(2,1)} %param.19) | copy-start | bytes 3145732
  24.2 17.3 %all-to-all-start.3 = ((bf16[8,112,128]{2,1,0:T(8,128)(2,1)}), bf16[8,112,128]{2,1,0:T(8,128)(2,1)S(1)}, u32[]{:S(2)}, u32[]{:S(2)}) async-start(bf16[8,112,128]{2,1,0:T(8,128)(2,1)} %bitcast.15), calls=%async_computation.3 | async-start | bytes 458752 | tf_op jit(solution)/shard_map/all_to_all | solution.py:23
  43.8 57.6 %all-to-all-start.2 = ((bf16[8,1024,256]{2,1,0:T(8,128)(2,1)}), bf16[8,1024,256]{2,1,0:T(8,128)(2,1)}, u32[]{:S(2)}, u32[]{:S(2)}) async-start(bf16[8,1024,256]{2,1,0:T(8,128)(2,1)} %broadcast_in_dim.34), calls=%async_computation.2 | async-start | bytes 8388608 | tf_op jit(solution)/shard_map/all_to_all | solution.py:23
  58.7 77.9 %collective-permute-start = (bf16[512,256]{0,1:T(8,128)(2,1)}, bf16[512,256]{0,1:T(8,128)(2,1)}, u32[]{:S(2)}, u32[]{:S(2)}) collective-permute-start(bf16[512,256]{0,1:T(8,128)(2,1)} %fusion.51), channel_id=1, source_target_pairs={{0,8},{8,16},{16,24},{24,32},{32,40},{40,48},{48,56},{56,64},{64,7... | collective-permute-start | bytes 786440 | tf_op jit(solution)/shard_map/ppermute | solution.py:119
  105.2 17.1 %all-to-all-start.4 = ((f32[4,224,256]{2,1,0:T(8,128)}), f32[4,224,256]{2,1,0:T(8,128)}, u32[]{:S(2)}, u32[]{:S(2)}) async-start(f32[4,224,256]{2,1,0:T(8,128)} %bitcast.124), calls=%async_computation.4 | async-start | bytes 1835008 | tf_op jit(solution)/shard_map/all_to_all | solution.py:23
  126.1 53.9 %all-to-all-start.5 = ((bf16[4,128,4096]{2,1,0:T(8,128)(2,1)}), bf16[4,128,4096]{2,1,0:T(8,128)(2,1)}, u32[]{:S(2)}, u32[]{:S(2)}) async-start(bf16[4,128,4096]{2,1,0:T(8,128)(2,1)} %broadcast_in_dim.35), calls=%async_computation.5 | async-start | bytes 8388608 | tf_op jit(solution)/shard_map/all_to_all | solution.py:23
  131.0 106.9 %all-gather.3.cloned.1.call-start = ((), (), s32[]{:S(2)}) async-start(), calls=%async_computation.12 | async-start | bytes 3784704 | tf_op jit(solution)/shard_map/all_gather | solution.py:102
  215.7 5.5 %copy-start.9 = (bf16[4,1024,128]{1,2,0:T(8,128)(2,1)S(1)}, bf16[4,1024,128]{1,2,0:T(8,128)(2,1)}, u32[]{:S(2)}) copy-start(bf16[4,1024,128]{1,2,0:T(8,128)(2,1)} %copy.46) | copy-start | bytes 3145732
  216.8 17.3 %all-to-all-start.8 = ((bf16[4,256,256]{2,1,0:T(8,128)(2,1)}), bf16[4,256,256]{2,1,0:T(8,128)(2,1)}, u32[]{:S(2)}, u32[]{:S(2)}) async-start(bf16[4,256,256]{2,1,0:T(8,128)(2,1)} %bitcast.30), calls=%async_computation.8 | async-start | bytes 1048576 | tf_op jit(solution)/shard_map/all_to_all | solution.py:23
  234.2 19.0 %all-to-all-start.1 = ((bf16[8,256,128]{2,1,0:T(8,128)(2,1)}), bf16[8,256,128]{2,1,0:T(8,128)(2,1)S(1)}, u32[]{:S(2)}, u32[]{:S(2)}) async-start(bf16[8,256,128]{2,1,0:T(8,128)(2,1)} %reshape.266), calls=%async_computation.1 | async-start | bytes 1048576 | tf_op jit(solution)/shard_map/all_to_all | solution.py:23
  248.5 10.3 %copy-start.14 = (bf16[128,1024]{1,0:T(8,128)(2,1)S(1)}, bf16[128,1024]{1,0:T(8,128)(2,1)}, u32[]{:S(2)}) copy-start(bf16[128,1024]{1,0:T(8,128)(2,1)} %param.27) | copy-start | bytes 786436
  253.9 19.8 %all-to-all-start.9 = ((bf16[8,256,256]{1,2,0:T(8,128)(2,1)}), bf16[8,256,256]{1,2,0:T(8,128)(2,1)S(1)}, u32[]{:S(2)}, u32[]{:S(2)}) async-start(bf16[8,256,256]{1,2,0:T(8,128)(2,1)} %fusion.25), calls=%async_computation.9 | async-start | bytes 2097152 | tf_op jit(solution)/shard_map/all_to_all | solution.py:23
  277.6 5.6 %copy-start.16 = (s32[2048]{0:T(1024)S(1)}, s32[2048]{0:T(1024)}, u32[]{:S(2)}) copy-start(s32[2048]{0:T(1024)} %param.21) | copy-start | bytes 24580
  277.6 54.3 %all-to-all-start = ((bf16[8,2,128,1024]{2,3,1,0:T(8,128)(2,1)}), bf16[8,2,128,1024]{2,3,1,0:T(8,128)(2,1)}, u32[]{:S(2)}, u32[]{:S(2)}) async-start(bf16[8,2,128,1024]{2,3,1,0:T(8,128)(2,1)} %broadcast_in_dim.30), calls=%async_computation | async-start | bytes 8388608 | tf_op jit(solution)/shard_map/all_to_all | solution.py:23
  285.0 7.4 %copy-start.3 = (bf16[2048,1024]{1,0:T(8,128)(2,1)S(1)}, bf16[2048,1024]{1,0:T(8,128)(2,1)}, u32[]{:S(2)}) copy-start(bf16[2048,1024]{1,0:T(8,128)(2,1)} %param.20) | copy-start | bytes 12582916
  285.0 11.0 %copy-start.10 = (pred[2048,302]{0,1:T(8,128)(4,1)S(1)}, pred[2048,302]{0,1:T(8,128)(4,1)}, u32[]{:S(2)}) copy-start(pred[2048,302]{0,1:T(8,128)(4,1)} %and_and_fusion) | copy-start | bytes 1855492
  287.5 7.4 %collective-permute-start.1 = (bf16[23,256]{1,0:T(8,128)(2,1)S(1)}, bf16[23,256]{1,0:T(8,128)(2,1)S(1)}, u32[]{:S(2)}, u32[]{:S(2)}) collective-permute-start(bf16[23,256]{1,0:T(8,128)(2,1)S(1)} %get-tuple-element.13), channel_id=1, source_target_pairs={{0,8},{8,16},{16,24},{24,32},{32,40},{40,48},{48,56},{56,64},{64,7... | collective-permute-start | bytes 35336 | tf_op jit(solution)/shard_map/ppermute | solution.py:46
  290.8 4.8 %collective-permute-start.2 = (bf16[23,256]{1,0:T(8,128)(2,1)S(1)}, bf16[23,256]{1,0:T(8,128)(2,1)S(1)}, u32[]{:S(2)}, u32[]{:S(2)}) collective-permute-start(bf16[23,256]{1,0:T(8,128)(2,1)S(1)} %get-tuple-element.14), channel_id=1, source_target_pairs={{8,0},{16,8},{24,16},{32,24},{40,32},{48,40},{56,48},{64,56},{72,6... | collective-permute-start | bytes 35336 | tf_op jit(solution)/shard_map/ppermute | solution.py:47
  332.0 13.7 %all-to-all-start.10 = ((bf16[8,256,128]{2,1,0:T(8,128)(2,1)}), bf16[8,256,128]{2,1,0:T(8,128)(2,1)S(1)}, u32[]{:S(2)}, u32[]{:S(2)}) async-start(bf16[8,256,128]{2,1,0:T(8,128)(2,1)} %copy.64), calls=%async_computation.10 | async-start | bytes 1048576 | tf_op jit(solution)/shard_map/all_to_all | solution.py:23
  340.5 21.2 %copy-start.1 = (bf16[1024,128]{1,0:T(8,128)(2,1)S(1)}, bf16[1024,128]{1,0:T(8,128)(2,1)}, u32[]{:S(2)}) copy-start(bf16[1024,128]{1,0:T(8,128)(2,1)} %param.25) | copy-start | bytes 786436
  (7 other events, 21.7 us)
Sparse Core Ops, SparseCore 0:
  23.5 58.3 all-gather.4
  134.4 87.2 all-gather.2
